TPU v7x, 256 devices: a whole 4x4x8 slice. The times are simulated.
256 devices in a mesh: grp: 8 (over z_lo, core), slab: 32 (over z_hi, x, y).
Axes of the slice: x: 4, y: 4, z: 8 (z_hi: 2, z_lo: 4; z = z_hi * 4 + z_lo), core: 2. Of those that a mesh axis runs over, the one named last changes fastest.
Arguments:
- occ_orbitals: bfloat16 [1024, 64, 4096], P(('grp', 'slab')), may hold values from -6 to 6
- vir_orbitals: bfloat16 [2048, 64, 4096], P(('grp', 'slab')), may hold values from -6 to 6
- pair_occ: int32 [8192], P(('grp', 'slab')), may hold values from 0 to 3
- pair_vir: int32 [8192], P(('grp', 'slab')), may hold values from 0 to 7
- sketch: bfloat16 [8192, 1024], P('grp'), may hold values from -6 to 6
Outputs:
- vertex: float32 [8192, 1024], P(('grp', 'slab'))
Inputs may be any that keep to these rules, and one draw needn't show every extreme that they name: `pair_occ`: an index into the 4 occupied orbitals held by the same device as the pair. `pair_vir`: an index into the 8 virtual orbitals held by the same device as the pair.
All inputs are finite; a program needn't handle non-finite values.
Results may differ from a plain program's by a relative error of at most 0.0057.
Values may be sent and summed in bfloat16 or wider, within the bound.
No kernel may reach another device: no remote copies, remote signals or barrier semaphores. Data moves between devices by JAX's collectives and lax.ppermute only.
A program may use at most 192 MiB of HBM per device.

v0:
```python
import math
import jax
import jax.numpy as jnp
from jax import lax
from jax.sharding import PartitionSpec as P

KYZ = 32
box_length = 10.0
screening = 1.0
epsilon = 1e-06


def real_basis(points, mode_count):
    grid_cells = jnp.arange(points, dtype=jnp.float32)[:, None]
    mode_index = jnp.arange(mode_count, dtype=jnp.int32)[None, :]
    frequency = (mode_index + 1) // 2
    phases = 2.0 * math.pi * grid_cells * frequency.astype(jnp.float32) / points
    values = jnp.where((mode_index % 2 == 1) | (mode_index == 0), jnp.cos(phases), jnp.sin(phases))
    factor = jnp.where(
        (mode_index == 0) | (2 * frequency == points),
        math.sqrt(1.0 / points),
        math.sqrt(2.0 / points),
    )
    return (values * factor).astype(jnp.bfloat16)


def coulomb_weight(modes_x, plane_count):
    freq_x = ((jnp.arange(modes_x, dtype=jnp.int32) + 1) // 2).astype(jnp.float32)
    freq_p = ((jnp.arange(plane_count, dtype=jnp.int32) + 1) // 2).astype(jnp.float32)
    plane_sq = (freq_p[:, None] * freq_p[:, None] + freq_p[None, :] * freq_p[None, :]).reshape(-1)
    summed_sq = plane_sq[:, None, None] + (freq_x * freq_x)[None, None, :]
    wave_sq = (2.0 * math.pi / box_length) ** 2 * summed_sq
    return jnp.sqrt(4.0 * math.pi / (wave_sq + screening * screening))


def pair_coefficients(occ_rows, vir_rows):
    pairs_dev = occ_rows.shape[0]
    grid_size = occ_rows.shape[1]
    basis_x = real_basis(grid_size, grid_size)
    basis_plane = real_basis(grid_size, KYZ)
    density = (occ_rows.astype(jnp.float32) * vir_rows.astype(jnp.float32)).astype(jnp.bfloat16)
    along_x = jnp.einsum(
        "pxs,xk->pks", density, basis_x, preferred_element_type=jnp.float32
    ).astype(jnp.bfloat16)
    planes = along_x.reshape(pairs_dev * grid_size, grid_size, grid_size)
    second = jnp.einsum(
        "ayz,zc->cya", planes, basis_plane, preferred_element_type=jnp.float32
    ).astype(jnp.bfloat16)
    along_y = jnp.einsum("cya,yb->bca", second, basis_plane, preferred_element_type=jnp.float32)
    weighted = along_y.reshape(KYZ * KYZ, pairs_dev, grid_size) * coulomb_weight(grid_size, KYZ)
    return weighted.astype(jnp.bfloat16)


def body(occ_orbitals, vir_orbitals, pair_occ, pair_vir, sketch):
    coulomb_rows = pair_coefficients(occ_orbitals[pair_occ], vir_orbitals[pair_vir])
    plane_modes, pairs_dev, modes_x = coulomb_rows.shape
    slab_count = lax.axis_size("slab")
    fields = sketch.shape[1]
    parcel = coulomb_rows.reshape(slab_count, plane_modes // slab_count, pairs_dev * modes_x)
    received = lax.all_to_all(parcel, "slab", split_axis=0, concat_axis=2, tiled=True)
    item_count = received.shape[1]
    grouped = received[0].reshape(item_count, -1, modes_x)
    partial_value = jnp.einsum("npk,pf->nkf", grouped, sketch, preferred_element_type=jnp.float32)
    partial_value, local_rows = (partial_value, received[0])
    flattened = partial_value.reshape(-1, fields)
    coef_count = plane_modes * modes_x
    portion = lax.psum_scatter(flattened, "grp", scatter_dimension=1, tiled=True)
    squares = lax.psum(jnp.sum(portion * portion, axis=0), "slab")
    scaled = (portion * lax.rsqrt(squares / coef_count + epsilon)).astype(jnp.bfloat16)
    field_basis = lax.all_gather(scaled, "grp", axis=1, tiled=True)
    slab_modes = field_basis.shape[0] // modes_x
    basis_rows = field_basis.reshape(slab_modes, modes_x, fields)
    gamma_rows = local_rows.reshape(slab_modes, -1, modes_x)
    summed = lax.psum_scatter(
        jnp.einsum("ypk,ykf->pf", gamma_rows, basis_rows, preferred_element_type=jnp.float32),
        "slab",
        scatter_dimension=0,
        tiled=True,
    )
    return summed * (1.0 / math.sqrt(coef_count))


def solution(mesh):
    return jax.shard_map(
        body,
        mesh=mesh,
        in_specs=(
            P(("grp", "slab"), None, None),
            P(("grp", "slab"), None, None),
            P(("grp", "slab")),
            P(("grp", "slab")),
            P("grp", None),
        ),
        out_specs=P(("grp", "slab"), None),
        check_vma=False,
    )
```

profile of v0, /device:TPU:32, one launch (start us, length us, event | category | flops | bytes accessed | tf_op | source)
XLA Modules:
  0.0 870.3 jit_solution(2158189540496240035)
XLA Ops:
  6.5 0.0 copy-start
  6.5 0.0 reduce-scatter.3.cloned.1.call-start
  6.6 0.8 compare_select_fusion.1
  7.4 0.7 compare_select_fusion
  8.1 0.0 copy-done
  8.1 7.2 gather_fusion
  15.3 9.4 %gather_fusion.1 = bf16[32,64,4096]{2,1,0:T(8,128)(2,1)} fusion(bf16[8,64,4096]{2,1,0:T(8,128)(2,1)} %param.6, s32[1024]{0:T(1024)S(1)} %pad_clamp_fusion), kind=kCustom, calls=%fused_computation.1 | custom fusion | bytes 33554560 | tf_op jit(solution)/shard_map/gather | solution.py:55
  24.7 23.4 %convert_bitcast_fusion = bf16[32,64,4096]{2,1,0:T(8,128)(2,1)} fusion(bf16[32,64,4096]{2,1,0:T(8,128)(2,1)} %gather_fusion.1, bf16[32,64,4096]{2,1,0:T(8,128)(2,1)} %gather_fusion, f32[64]{0:T(128)S(1)} %get-tuple-element.5, f32[64]{0:T(128)S(1)} %fusion.20, f32[64]{0:T(128)S(1)} %get-tuple-element.6, pred[64]{0:T(512)(128)(4,1)S(1)} %compare_or_fusion), kind=kOutput, calls=%fused_computation.6 | convolution fusion | flops 1115705344 | bytes 50332480 | tf_op jit(solution)/shard_map/pxs,xk->pks/dot_general | solution.py:42
  48.2 46.0 %reshape.261 = bf16[2048,64,64]{2,1,0:T(8,128)(2,1)} reshape(bf16[32,64,4096]{2,1,0:T(8,128)(2,1)} %convert_bitcast_fusion) | data formatting | bytes 33554432 | tf_op jit(solution)/shard_map/reshape | solution.py:45
  94.2 0.1 broadcast_add_fusion
  94.2 0.1 add.182
  94.3 0.2 divide_sqrt_fusion
  94.5 0.2 copy.19
  94.7 6.8 mul.166
  101.5 14.8 %mul.167 = f32[32,32,2048]{2,1,0:T(8,128)} reshape(f32[1024,32,64]{2,1,0:T(8,128)} %mul.166) | data formatting | bytes 16777216 | tf_op jit(solution)/shard_map/mul | solution.py:50
  116.3 0.0 copy-start.2
  116.3 75.2 %convert_bitcast_fusion.1 = bf16[32,64,2048]{2,0,1:T(8,128)(2,1)} fusion(bf16[2048,64,64]{2,1,0:T(8,128)(2,1)} %reshape.261, f32[32]{0:T(128)S(1)} %or_select_fusion.1, f32[32]{0:T(128)S(1)} %fusion.21, f32[64]{0:T(128)S(1)} %get-tuple-element.6, pred[32]{0:T(512)(128)(4,1)S(1)} %compare_or_fusion.1), kind=kOutput, calls=%fused_computation.11 | convolution fusion | flops 541075456 | bytes 25166368 | tf_op jit(solution)/shard_map/ayz,zc->cya/dot_general | solution.py:46
  191.5 0.0 copy-done.2
  191.5 18.1 %fusion.3 = bf16[32,32,2048]{2,0,1:T(8,128)(2,1)S(1)} fusion(f32[32,32,2048]{2,1,0:T(8,128)S(1)} %copy-done.2, bf16[32,64,2048]{2,0,1:T(8,128)(2,1)} %convert_bitcast_fusion.1, f32[32]{0:T(128)S(1)} %or_select_fusion.1, f32[32]{0:T(128)S(1)} %fusion.21, f32[64]{0:T(128)S(1)} %get-tuple-element.6, pred[32]{0:T(512)(128)(4,1)S(1)} %compare_or_fusion.1), kind=kOutput, calls=%fused_computation.8 | convolution fusion | flops 272640000 | bytes 20972064 | tf_op jit(solution)/shard_map/cya,yb->bca/dot_general | solution.py:49
  209.7 2.3 copy.21
  212.0 111.3 %all_to_all.15 = bf16[32,32,2048]{2,1,0:T(8,128)(2,1)S(1)} all-to-all(bf16[32,32,2048]{2,1,0:T(8,128)(2,1)S(1)} %copy.21), channel_id=1, replica_groups=mesh['grp'=8,'slab'=32] {'slab'}, dimensions={0} | all-to-all | bytes 8388608 | tf_op jit(solution)/shard_map/all_to_all | solution.py:60
  323.3 4.3 copy.22
  327.5 12.9 %reshape_squeeze.4 = bf16[32,1024,64]{2,1,0:T(8,128)(2,1)} reshape(bf16[1,32,32,2048]{3,2,1,0:T(8,128)(2,1)} %copy.22) | data formatting | bytes 8388608 | tf_op jit(solution)/shard_map/reshape;squeeze | solution.py:73
  340.4 0.0 copy-start.3
  340.4 8.7 copy.23
  349.1 0.0 copy-done.3
  349.1 8.9 %fusion.27 = f32[2048,1024]{1,0:T(8,128)} fusion(bf16[2048,1024]{1,0:T(8,128)(2,1)} %bitcast.27, bf16[1024,1024]{1,0:T(8,128)(2,1)S(1)} %copy-done.3), kind=kOutput, calls=%fused_computation.56 | convolution fusion | flops 4294967296 | bytes 14680064 | tf_op jit(solution)/shard_map/npk,pf->nkf/dot_general | solution.py:63
  358.0 0.0 reduce-scatter.3.cloned.1.call-update
  358.0 0.0 all-gather.2.cloned.1.call-start
  358.1 86.6 %reduce-scatter.3.cloned.1.call-done = f32[2048,128]{1,0:T(8,128)} async-done(((f32[2048,1024]{1,0:T(8,128)}), f32[2048,128]{1,0:T(8,128)}) %reduce-scatter.3.cloned.1.call-update) | async-done | bytes 1048592 | tf_op jit(solution)/shard_map/reduce_scatter | solution.py:67
  444.6 1.5 multiply_reduce_fusion
  446.1 118.9 %psum.7 = f32[128]{0:T(128)S(1)} all-reduce(f32[128]{0:T(128)S(1)} %multiply_reduce_fusion), channel_id=1, replica_groups=mesh['grp'=8,'slab'=32] {'slab'}, use_global_device_ids=true, to_apply=%region_2.3 | all-reduce | flops 128 | bytes 1024 | tf_op jit(solution)/shard_map/psum | solution.py:68
  565.0 2.1 multiply_convert_fusion.4
  567.1 0.0 all-gather.2.cloned.1.call-update
  567.1 0.0 reduce-scatter.5.cloned.1.call-start
  567.2 46.7 %all-gather.2.cloned.1.call-done = bf16[2048,1024]{1,0:T(8,128)(2,1)} async-done(((bf16[2048,128]{1,0:T(8,128)(2,1)}), bf16[2048,1024]{1,0:T(8,128)(2,1)}) %all-gather.2.cloned.1.call-update) | async-done | bytes 4194320 | tf_op jit(solution)/shard_map/all_gather | solution.py:70
  613.8 0.0 copy-start.1
  613.8 9.7 %convolution_bitcast_fusion = f32[1024,1024]{1,0:T(8,128)} fusion(bf16[32,1024,64]{2,1,0:T(8,128)(2,1)} %reshape_squeeze.4, bf16[32,64,1024]{2,1,0:T(8,128)(2,1)} %bitcast.28), kind=kOutput, calls=%fused_computation.12 | convolution fusion | flops 4294967296 | bytes 12582912 | tf_op jit(solution)/shard_map/ypk,ykf->pf/dot_general | solution.py:75
  623.5 0.0 reduce-scatter.5.cloned.1.call-update
  623.5 238.5 %reduce-scatter.5.cloned.1.call-done = f32[32,1024]{1,0:T(8,128)} async-done(((f32[1024,1024]{1,0:T(8,128)}), f32[32,1024]{1,0:T(8,128)}) %reduce-scatter.5.cloned.1.call-update) | async-done | bytes 131088 | tf_op jit(solution)/shard_map/reduce_scatter | solution.py:74
  862.0 1.6 broadcast_multiply_fusion
  863.6 0.0 copy-done.1
  (11 shorter events, 0.1 us)
Async XLA Ops:
  6.5 1.6 copy-start
  6.5 438.1 %reduce-scatter.3.cloned.1.call-start = ((), (), s32[]{:S(2)}) async-start(), calls=%async_computation.3 | async-start | bytes 9437184 | tf_op jit(solution)/shard_map/reduce_scatter | solution.py:67
  116.3 75.2 %copy-start.2 = (f32[32,32,2048]{2,1,0:T(8,128)S(1)}, f32[32,32,2048]{2,1,0:T(8,128)}, u32[]{:S(2)}) copy-start(f32[32,32,2048]{2,1,0:T(8,128)} %mul.167) | copy-start | bytes 25165828
  340.4 8.7 copy-start.3
  358.0 255.8 %all-gather.2.cloned.1.call-start = ((), (), s32[]{:S(2)}) async-start(), calls=%async_computation.4 | async-start | bytes 4718592 | tf_op jit(solution)/shard_map/all_gather | solution.py:70
  567.1 294.9 %reduce-scatter.5.cloned.1.call-start = ((), (), s32[]{:S(2)}) async-start(), calls=%async_computation.5 | async-start | bytes 4325376 | tf_op jit(solution)/shard_map/reduce_scatter | solution.py:74
  613.8 249.8 %copy-start.1 = (bf16[4,64,4096]{2,1,0:T(8,128)(2,1)S(1)}, bf16[4,64,4096]{2,1,0:T(8,128)(2,1)}, u32[]{:S(2)}) copy-start(bf16[4,64,4096]{2,1,0:T(8,128)(2,1)} %param.5) | copy-start | bytes 6291460
Sparse Core Ops, SparseCore 0:
  358.1 86.4 reduce-scatter.2
  567.2 46.5 all-gather.1
  623.7 238.3 reduce-scatter.4
where the time goes:
time: 878 us; the launch traced here: 870 us
  waiting for transfers between devices  372 us (42%)
  blocking collectives  230 us (26%)
  matrix products  135 us (15%)
  local copies, waits for them, and re-layouts  113 us (13%)
  between operations  13.4 us (2%)
    reduce_scatter x1, waiting for transfers between devices, body(): lax.psum_scatter(jnp.einsum('ypk,ykf->pf', gamma_rows, basis_rows, prefer...  238 us
    psum x1, blocking collectives, body(): squares = lax.psum(jnp.sum(portion * portion, axis=0), 'slab')  119 us
    all_to_all x1, blocking collectives, body(): lax.all_to_all(parcel, 'slab', split_axis=0, concat_axis=2, tiled=True)  111 us
    reduce_scatter x1, waiting for transfers between devices, body(): lax.psum_scatter(flattened, 'grp', scatter_dimension=1, tiled=True)  86.6 us
    dot_general x1, matrix products, pair_coefficients(): jnp.einsum('ayz,zc->cya', planes, basis_plane, preferred_element_type=jnp...  75.2 us
    all_gather x1, waiting for transfers between devices, body(): field_basis = lax.all_gather(scaled, 'grp', axis=1, tiled=True)  46.7 us
    reshape x1, local copies, waits for them, and re-layouts, pair_coefficients(): planes = along_x.reshape(pairs_dev * grid_size, grid_size, grid_size)  46 us
    dot_general x1, matrix products, pair_coefficients(): jnp.einsum('pxs,xk->pks', density, basis_x, preferred_element_type=jnp.fl...  23.4 us
  transfers between devices with their start and end apart: 3, of which 3 were waited for; matrix products, arithmetic and copies ran while one was open for 0% of the time, Pallas kernels for 0%

commit v1 on v0

--- a/solution.py
+++ b/solution.py
@@ -67,7 +67,9 @@
     portion = lax.psum_scatter(flattened, "grp", scatter_dimension=1, tiled=True)
     squares = lax.psum(jnp.sum(portion * portion, axis=0), "slab")
     scaled = (portion * lax.rsqrt(squares / coef_count + epsilon)).astype(jnp.bfloat16)
-    field_basis = lax.all_gather(scaled, "grp", axis=1, tiled=True)
+    field_basis = jnp.concatenate(
+        lax.all_to_all(jnp.stack([scaled] * lax.axis_size("grp")), "grp", 0, 0), axis=1
+    )
     slab_modes = field_basis.shape[0] // modes_x
     basis_rows = field_basis.reshape(slab_modes, modes_x, fields)
     gamma_rows = local_rows.reshape(slab_modes, -1, modes_x)

time: 878 us -> 951 us (1.083)
  blocking collectives: 230 us -> 325 us
  waiting for transfers between devices: 372 us -> 320 us
  local copies, waits for them, and re-layouts: 113 us -> 134 us
    all_to_all x0 -> x1, blocking collectives: none -> 95 us  [body(): lax.all_to_all(jnp.stack([scaled] * lax.axis_size('grp')), 'grp', 0, 0)]
    all_gather x1 -> x0, waiting for transfers between devices: 46.7 us -> none  [body(): field_basis = lax.all_gather(scaled, 'grp', axis=1, tiled=True)]
    reshape x0 -> x1, local copies, waits for them, and re-layouts: none -> 13.2 us  [body(): jnp.concatenate(lax.all_to_all(jnp.stack([scaled] * lax.axis_size('grp'))...]
  transfers between devices with their start and end apart: 3 -> 2, of which waited for: 3 -> 2; matrix products, arithmetic and copies ran while one was open for 0% -> 0% of each run, Pallas kernels for 0% -> 0%
where the time goes in v1:
time: 951 us; the launch traced here: 943 us
  blocking collectives  325 us (34%)
  waiting for transfers between devices  320 us (34%)
  matrix products  144 us (15%)
  local copies, waits for them, and re-layouts  134 us (14%)
  between operations  14 us (1%)
    reduce_scatter x1, waiting for transfers between devices, body(): lax.psum_scatter(jnp.einsum('ypk,ykf->pf', gamma_rows, basis_rows, prefer...  233 us
    psum x1, blocking collectives, body(): squares = lax.psum(jnp.sum(portion * portion, axis=0), 'slab')  119 us
    all_to_all x1, blocking collectives, body(): lax.all_to_all(parcel, 'slab', split_axis=0, concat_axis=2, tiled=True)  111 us
    all_to_all x1, blocking collectives, body(): lax.all_to_all(jnp.stack([scaled] * lax.axis_size('grp')), 'grp', 0, 0)  95 us
    reduce_scatter x1, waiting for transfers between devices, body(): lax.psum_scatter(flattened, 'grp', scatter_dimension=1, tiled=True)  86.6 us
    dot_general x1, matrix products, pair_coefficients(): jnp.einsum('ayz,zc->cya', planes, basis_plane, preferred_element_type=jnp...  83.4 us
    reshape x1, local copies, waits for them, and re-layouts, pair_coefficients(): planes = along_x.reshape(pairs_dev * grid_size, grid_size, grid_size)  46 us
    dot_general x1, matrix products, pair_coefficients(): jnp.einsum('pxs,xk->pks', density, basis_x, preferred_element_type=jnp.fl...  23.4 us
  transfers between devices with their start and end apart: 2, of which 2 were waited for; matrix products, arithmetic and copies ran while one was open for 0% of the time, Pallas kernels for 0%

profile of v1, /device:TPU:32, one launch (start us, length us, event | category | flops | bytes accessed | tf_op | source)
XLA Modules:
  0.0 942.6 jit_solution(14064590833864545182)
XLA Ops:
  6.5 0.0 copy-start
  6.5 0.0 reduce-scatter.3.cloned.1.call-start
  6.6 0.8 compare_select_fusion.1
  7.4 0.7 compare_select_fusion
  8.1 0.0 copy-done
  8.1 7.2 gather_fusion
  15.3 9.4 gather_fusion.1
  24.7 23.4 %convert_bitcast_fusion = bf16[32,64,4096]{2,1,0:T(8,128)(2,1)} fusion(bf16[32,64,4096]{2,1,0:T(8,128)(2,1)} %gather_fusion.1, bf16[32,64,4096]{2,1,0:T(8,128)(2,1)} %gather_fusion, f32[64]{0:T(128)S(1)} %get-tuple-element.5, f32[64]{0:T(128)S(1)} %fusion.20, f32[64]{0:T(128)S(1)} %get-tuple-element.6, pred[64]{0:T(512)(128)(4,1)S(1)} %compare_or_fusion), kind=kOutput, calls=%fused_computation.6 | convolution fusion | flops 1115705344 | bytes 50332480 | tf_op jit(solution)/shard_map/pxs,xk->pks/dot_general | solution.py:42
  48.1 46.0 %reshape.263 = bf16[2048,64,64]{2,1,0:T(8,128)(2,1)} reshape(bf16[32,64,4096]{2,1,0:T(8,128)(2,1)} %convert_bitcast_fusion) | data formatting | bytes 33554432 | tf_op jit(solution)/shard_map/reshape | solution.py:45
  94.1 0.1 broadcast_add_fusion
  94.2 0.1 add.182
  94.3 0.2 divide_sqrt_fusion
  94.5 0.2 copy.20
  94.7 6.8 mul.166
  101.4 14.8 %mul.167 = f32[32,32,2048]{2,1,0:T(8,128)} reshape(f32[1024,32,64]{2,1,0:T(8,128)} %mul.166) | data formatting | bytes 16777216 | tf_op jit(solution)/shard_map/mul | solution.py:50
  116.2 0.0 copy-start.2
  116.2 83.4 %convert_bitcast_fusion.1 = bf16[32,64,2048]{2,0,1:T(8,128)(2,1)} fusion(bf16[2048,64,64]{2,1,0:T(8,128)(2,1)} %reshape.263, f32[32]{0:T(128)S(1)} %or_select_fusion.1, f32[32]{0:T(128)S(1)} %fusion.21, f32[64]{0:T(128)S(1)} %get-tuple-element.6, pred[32]{0:T(512)(128)(4,1)S(1)} %compare_or_fusion.1), kind=kOutput, calls=%fused_computation.11 | convolution fusion | flops 541075456 | bytes 25166368 | tf_op jit(solution)/shard_map/ayz,zc->cya/dot_general | solution.py:46
  199.7 0.0 copy-done.2
  199.7 18.2 %fusion.3 = bf16[32,32,2048]{2,0,1:T(8,128)(2,1)S(1)} fusion(f32[32,32,2048]{2,1,0:T(8,128)S(1)} %copy-done.2, bf16[32,64,2048]{2,0,1:T(8,128)(2,1)} %convert_bitcast_fusion.1, f32[32]{0:T(128)S(1)} %or_select_fusion.1, f32[32]{0:T(128)S(1)} %fusion.21, f32[64]{0:T(128)S(1)} %get-tuple-element.6, pred[32]{0:T(512)(128)(4,1)S(1)} %compare_or_fusion.1), kind=kOutput, calls=%fused_computation.8 | convolution fusion | flops 272640000 | bytes 20972064 | tf_op jit(solution)/shard_map/cya,yb->bca/dot_general | solution.py:49
  217.9 2.3 copy.22
  220.2 111.3 %all_to_all.20 = bf16[32,32,2048]{2,1,0:T(8,128)(2,1)S(1)} all-to-all(bf16[32,32,2048]{2,1,0:T(8,128)(2,1)S(1)} %copy.22), channel_id=1, replica_groups=mesh['grp'=8,'slab'=32] {'slab'}, dimensions={0} | all-to-all | bytes 8388608 | tf_op jit(solution)/shard_map/all_to_all | solution.py:60
  331.4 4.3 copy.23
  335.7 12.9 %reshape_squeeze.4 = bf16[32,1024,64]{2,1,0:T(8,128)(2,1)} reshape(bf16[1,32,32,2048]{3,2,1,0:T(8,128)(2,1)} %copy.23) | data formatting | bytes 8388608 | tf_op jit(solution)/shard_map/reshape;squeeze | solution.py:75
  348.6 0.0 copy-start.3
  348.6 8.7 copy.24
  357.3 0.0 copy-done.3
  357.3 8.9 fusion.27
  366.2 0.0 reduce-scatter.3.cloned.1.call-update
  366.2 0.0 reduce-scatter.5.cloned.1.call-start
  366.3 86.6 %reduce-scatter.3.cloned.1.call-done = f32[2048,128]{1,0:T(8,128)} async-done(((f32[2048,1024]{1,0:T(8,128)}), f32[2048,128]{1,0:T(8,128)}) %reduce-scatter.3.cloned.1.call-update) | async-done | bytes 1048592 | tf_op jit(solution)/shard_map/reduce_scatter | solution.py:67
  452.8 1.5 multiply_reduce_fusion
  454.3 119.1 %psum.7 = f32[128]{0:T(128)S(1)} all-reduce(f32[128]{0:T(128)S(1)} %multiply_reduce_fusion), channel_id=1, replica_groups=mesh['grp'=8,'slab'=32] {'slab'}, use_global_device_ids=true, to_apply=%region_2.3 | all-reduce | flops 128 | bytes 1024 | tf_op jit(solution)/shard_map/psum | solution.py:68
  573.4 1.3 multiply_convert_fusion.4
  574.7 0.5 stack.2
  575.3 95.0 %all_to_all.21 = bf16[8,2048,128]{2,1,0:T(8,128)(2,1)S(1)} all-to-all(bf16[8,2048,128]{2,1,0:T(8,128)(2,1)S(1)} %stack.2), channel_id=1, replica_groups=mesh['grp'=8,'slab'=32] {'grp'}, dimensions={0} | all-to-all | bytes 8388608 | tf_op jit(solution)/shard_map/all_to_all | solution.py:71
  670.3 13.2 %copy.25 = bf16[2048,8,128]{2,1,0:T(8,128)(2,1)} copy(bf16[2048,8,128]{2,0,1:T(8,128)(2,1)S(1)} %bitcast.27) | data formatting | bytes 8388608 | tf_op jit(solution)/shard_map/reshape | solution.py:70
  683.5 7.3 reshape_reshape.3
  690.8 0.0 copy-start.1
  690.8 9.7 %convolution_bitcast_fusion = f32[1024,1024]{1,0:T(8,128)} fusion(bf16[32,1024,64]{2,1,0:T(8,128)(2,1)} %reshape_squeeze.4, bf16[32,64,1024]{2,1,0:T(8,128)(2,1)} %reshape_reshape.3), kind=kOutput, calls=%fused_computation.12 | convolution fusion | flops 4294967296 | bytes 12582912 | tf_op jit(solution)/shard_map/ypk,ykf->pf/dot_general | solution.py:77
  700.5 0.0 reduce-scatter.5.cloned.1.call-update
  700.5 233.2 %reduce-scatter.5.cloned.1.call-done = f32[32,1024]{1,0:T(8,128)} async-done(((f32[1024,1024]{1,0:T(8,128)}), f32[32,1024]{1,0:T(8,128)}) %reduce-scatter.5.cloned.1.call-update) | async-done | bytes 131088 | tf_op jit(solution)/shard_map/reduce_scatter | solution.py:76
  933.7 1.6 broadcast_multiply_fusion
  935.3 0.0 copy-done.1
  (11 shorter events, 0.1 us)
Async XLA Ops:
  6.5 1.6 copy-start
  6.5 446.3 %reduce-scatter.3.cloned.1.call-start = ((), (), s32[]{:S(2)}) async-start(), calls=%async_computation.4 | async-start | bytes 9437184 | tf_op jit(solution)/shard_map/reduce_scatter | solution.py:67
  116.2 83.4 %copy-start.2 = (f32[32,32,2048]{2,1,0:T(8,128)S(1)}, f32[32,32,2048]{2,1,0:T(8,128)}, u32[]{:S(2)}) copy-start(f32[32,32,2048]{2,1,0:T(8,128)} %mul.167) | copy-start | bytes 25165828
  348.6 8.7 copy-start.3
  366.2 567.5 %reduce-scatter.5.cloned.1.call-start = ((), (), s32[]{:S(2)}) async-start(), calls=%async_computation.5 | async-start | bytes 4325376 | tf_op jit(solution)/shard_map/reduce_scatter | solution.py:76
  690.8 244.5 %copy-start.1 = (bf16[4,64,4096]{2,1,0:T(8,128)(2,1)S(1)}, bf16[4,64,4096]{2,1,0:T(8,128)(2,1)}, u32[]{:S(2)}) copy-start(bf16[4,64,4096]{2,1,0:T(8,128)(2,1)} %param.5) | copy-start | bytes 6291460
Sparse Core Ops, SparseCore 0:
  366.3 86.4 reduce-scatter.2
  700.7 232.9 reduce-scatter.4
